TPU v7x, 256 devices: a whole 4x4x8 slice. The times are simulated.
256 devices in a mesh: batch: 8 (over x, core), hidden: 4 (over z_hi), solver: 8 (over z_lo, y).
Axes of the slice: x: 4, y: 4, z: 8 (z_hi: 4, z_lo: 2; z = z_hi * 2 + z_lo), core: 2. Of those that a mesh axis runs over, the one named last changes fastest.
Arguments:
- activations: bfloat16 [2048, 4096], P('batch', ('hidden', 'solver')), may hold values from -16 to 16, as said below
- cotangent: bfloat16 [8192, 2048], P(('hidden', 'solver'), 'batch'), may hold values from -0.13183594 to 0.13183594
- weight: bfloat16 [4096, 8192], P(('hidden', 'solver'), 'batch'), may hold values from -0.09375 to 0.09375
- left_old: float32 [4, 8, 1024, 1024], P('hidden', 'batch'), may hold values from -0.001953125 to 2.0019531, as said below
- right_old: float32 [4, 8, 1024, 1024], P('hidden', 'batch'), may hold values from -0.001953125 to 2.0019531, as said below
Outputs:
- first_out: bfloat16 [8192, 2048], P(('hidden', 'solver'), 'batch')
- new_left: float32 [4, 8, 1024, 1024], P('hidden', 'batch', 'solver')
- new_right: float32 [4, 8, 1024, 1024], P('hidden', 'batch', 'solver')
- direction: float32 [4096, 8192], P(('hidden', 'solver'), 'batch')
- second_out: bfloat16 [8192, 2048], P(('hidden', 'solver'), 'batch')
Inputs may be any that keep to these rules, and one draw needn't show every extreme that they name: `activations`: in the hidden draw each feature carries its own scale. `left_old`: every block is symmetric, its diagonal is positive and larger than the sum of the magnitudes of the rest of its row. `right_old`: every block is symmetric, its diagonal is positive and larger than the sum of the magnitudes of the rest of its row.
All inputs are finite; a program needn't handle non-finite values. Where the computation divides by a largest or mean magnitude, that divisor is 1e-20 or more.
Results may differ from a plain program's by a relative error of at most 0.017.
Values may be sent and summed in bfloat16 or wider, within the bound.
No kernel may reach another device: no remote copies, remote signals or barrier semaphores. Data moves between devices by JAX's collectives and lax.ppermute only.
A program may use at most 128 MiB of HBM per device.

v0:
```python
import jax
import jax.numpy as jnp
from jax import lax
from jax.sharding import PartitionSpec as P

BLOCK = 1024
STAT_DECAY = 0.8
LEARN_RATE = 0.005
EPSILON = 1e-06


def in_order(blocks, dim):
    blocks = jnp.moveaxis(blocks, 0, dim)
    shape = blocks.shape
    return blocks.reshape(*shape[:dim], shape[dim] * shape[dim + 1], *shape[dim + 2 :])


def sent_to_all(shard, axis):
    copies = jnp.broadcast_to(shard, (lax.axis_size(axis), *shard.shape))
    return lax.all_to_all(copies, axis, split_axis=0, concat_axis=0, tiled=True)


def gather_directly(shard, axis, dim):
    return in_order(sent_to_all(shard, axis), dim)


def cut_along(shard, dim, peers):
    before, after = (shard.shape[:dim], shard.shape[dim + 1 :])
    return jnp.moveaxis(shard.reshape(*before, peers, -1, *after), dim, 0)


def summed_on_arrival(shard, axis, dim):
    blocks = cut_along(shard, dim, lax.axis_size(axis))
    arrived = lax.all_to_all(blocks, axis, split_axis=0, concat_axis=0, tiled=True)
    return arrived.astype(jnp.float32).sum(axis=0)


def taken_together(shard, axis):
    everything = sent_to_all(shard, axis)
    return jnp.sum(everything, axis=0)


def product(left_mat, right_mat):
    return jnp.einsum("bij,bjk->bik", left_mat, right_mat, preferred_element_type=jnp.float32)


def prepare(factor):
    identity = jnp.eye(BLOCK, dtype=jnp.float32)
    scaled = 2.5 / (jnp.max(jnp.sum(jnp.abs(factor), axis=2), axis=1) + EPSILON)
    moment = scaled[:, None, None] * factor
    newton_step = (5.0 * identity - moment) * 0.25
    return (scaled, moment, newton_step)


def transposed_product(weight_cols, acts):
    return lax.dot_general(
        weight_cols, acts, (((0,), (1,)), ((), ())), preferred_element_type=jnp.float32
    )


def body(activations, cotangent, weight, left_old, right_old):
    rows_here = weight.shape[0]
    nblocks = weight.shape[1] // BLOCK
    weight_rows = gather_directly(weight, "batch", 1)
    gathered = lax.all_gather(activations, ("hidden", "solver"), axis=1, tiled=True)
    weight_cols = lax.all_to_all(
        weight_rows, ("hidden", "solver"), split_axis=1, concat_axis=0, tiled=True
    )
    first_sum = transposed_product(weight_cols, gathered)
    first_out = first_sum.astype(jnp.bfloat16)
    cotangent_all = lax.all_gather(cotangent, ("hidden", "solver"), axis=0, tiled=True)
    grad_local = summed_on_arrival(
        jnp.dot(cotangent_all, activations, preferred_element_type=jnp.float32).astype(
            jnp.bfloat16
        ),
        "batch",
        0,
    ).astype(jnp.bfloat16)
    grad_blocks = grad_local.reshape(nblocks, BLOCK, rows_here)
    grad_full = gather_directly(grad_blocks, "solver", 2)
    gram_left = jnp.einsum("bnm,bnk->bmk", grad_full, grad_full, preferred_element_type=jnp.float32)
    gram_right = jnp.einsum(
        "bnm,bkm->bnk", grad_full, grad_full, preferred_element_type=jnp.float32
    )
    left_all = STAT_DECAY * left_old[0] + (1.0 - STAT_DECAY) / BLOCK * gram_left
    right_all = STAT_DECAY * right_old[0] + (1.0 - STAT_DECAY) / BLOCK * gram_right
    first_row = lax.axis_index("solver") * rows_here
    new_left = lax.dynamic_slice_in_dim(left_all, first_row, rows_here, 1)[None]
    new_right = lax.dynamic_slice_in_dim(right_all, first_row, rows_here, 1)[None]
    scale_left, moment_left, step_left = prepare(left_all)
    own_rows = lax.dynamic_slice_in_dim(step_left, first_row, rows_here, 1)
    power_rows = product(
        product(product(product(own_rows, step_left), step_left), step_left), moment_left
    )
    row_index = lax.broadcasted_iota(jnp.int32, (rows_here, BLOCK), 0) + first_row
    col_index = lax.broadcasted_iota(jnp.int32, (rows_here, BLOCK), 1)
    eye_rows = (row_index == col_index).astype(jnp.float32)
    next_rows = (5.0 * eye_rows - power_rows) * 0.25
    root_rows = (scale_left**0.25)[:, None, None] * product(next_rows, step_left)
    grad_float = grad_full.astype(jnp.float32)
    mixed_rows = jnp.einsum(
        "brm,bnm->brn", root_rows, grad_float, preferred_element_type=jnp.float32
    )
    scale_right, moment_right, step_right = prepare(right_all)
    turned = product(mixed_rows, step_right)
    power_right = product(
        product(product(product(product(turned, step_right), step_right), step_right), step_right),
        moment_right,
    )
    update = (scale_right**0.25)[:, None, None] * ((5.0 * turned - power_right) * 0.25)
    squares = taken_together(jnp.sum(update * update, axis=(1, 2)), "solver")
    spread = jnp.sqrt(squares / (BLOCK * BLOCK) + EPSILON)
    scaled_update = update / spread[:, None, None]
    direction = jnp.transpose(scaled_update, (1, 0, 2)).reshape(rows_here, nblocks * BLOCK)
    new_weight = (weight.astype(jnp.float32) - LEARN_RATE * direction).astype(jnp.bfloat16)
    new_rows = gather_directly(new_weight, "batch", 1)
    new_cols = lax.all_to_all(
        new_rows, ("hidden", "solver"), split_axis=1, concat_axis=0, tiled=True
    )
    second_sum = transposed_product(new_cols, gathered)
    second_out = second_sum.astype(jnp.bfloat16)
    return (first_out, new_left, new_right, direction, second_out)


def solution(mesh):
    in_specs = (
        P("batch", ("hidden", "solver")),
        P(("hidden", "solver"), "batch"),
        P(("hidden", "solver"), "batch"),
        P("hidden", "batch", None, None),
        P("hidden", "batch", None, None),
    )
    out_specs = (
        P(("hidden", "solver"), "batch"),
        P("hidden", "batch", "solver", None),
        P("hidden", "batch", "solver", None),
        P(("hidden", "solver"), "batch"),
        P(("hidden", "solver"), "batch"),
    )
    return jax.shard_map(body, mesh=mesh, in_specs=in_specs, out_specs=out_specs, check_vma=False)
```

profile of v0, /device:TPU:24, one launch (start us, length us, event | category | flops | bytes accessed | tf_op | source)
XLA Modules:
  0.0 407.6 jit_solution(7480275849484787042)
XLA Ops:
  7.2 0.0 all-gather.5.cloned.1.call-start
  7.2 0.7 all-gather.5.cloned.1.call-update
  7.9 85.3 %all-gather.5.cloned.1.call-done = bf16[8192,256]{1,0:T(8,128)(2,1)} async-done(((bf16[256,256]{1,0:T(8,128)(2,1)}), bf16[8192,256]{1,0:T(8,128)(2,1)}) %all-gather.5.cloned.1.call-update) | async-done | bytes 4194320 | tf_op jit(solution)/shard_map/all_gather | solution.py:71
  93.2 3.4 convolution_convert_fusion
  96.7 31.6 %all_to_all.64 = bf16[8,1024,128]{2,1,0:T(8,128)(2,1)S(1)} all-to-all(bf16[8,1024,128]{2,1,0:T(8,128)(2,1)S(1)} %bitcast.48), channel_id=1, replica_groups=mesh['batch'=8,'hidden'=4,'solver'=8] {'batch'}, dimensions={0} | all-to-all | bytes 4194304 | tf_op jit(solution)/shard_map/all_to_all | solution.py:34
  128.3 0.0 copy-start.3
  128.3 0.4 reduce_sum.48
  128.7 1.6 broadcast_in_dim.13
  130.3 6.3 %all-to-all-start.3 = ((bf16[8,1,1024,128]{3,2,1,0:T(8,128)(2,1)}), bf16[8,1,1024,128]{3,2,1,0:T(8,128)(2,1)S(1)}, u32[]{:S(2)}, u32[]{:S(2)}) async-start(bf16[8,1,1024,128]{3,2,1,0:T(8,128)(2,1)} %broadcast_in_dim.13), calls=%async_computation.3 | async-start | bytes 4194304 | tf_op jit(solution)/shard_map/all_to_all | solution.py:20
  136.6 0.0 copy-done.3
  136.6 0.2 copy.41
  136.8 5.4 %copy.43 = f32[1,1,1024,1024]{2,3,1,0:T(8,128)} copy(f32[1,1,1024,1024]{3,2,1,0:T(8,128)} %param.8) | data formatting | bytes 8388608 | tf_op args[3]
  142.2 5.3 %copy.47 = f32[1,1,1024,1024]{2,3,1,0:T(8,128)} copy(f32[1,1,1024,1024]{3,2,1,0:T(8,128)} %param.9) | data formatting | bytes 8388608 | tf_op args[4]
  147.5 13.4 %all-to-all-done.3 = bf16[8,1,1024,128]{3,2,1,0:T(8,128)(2,1)S(1)} async-done(((bf16[8,1,1024,128]{3,2,1,0:T(8,128)(2,1)}), bf16[8,1,1024,128]{3,2,1,0:T(8,128)(2,1)S(1)}, u32[]{:S(2)}, u32[]{:S(2)}) %all-to-all-start.3) | async-done | bytes 2097184 | tf_op jit(solution)/shard_map/all_to_all | solution.py:20
  160.9 0.0 copy-start
  160.9 1.8 broadcast_in_dim.12
  162.8 4.5 %all-to-all-start = ((bf16[8,128,1024]{1,2,0:T(8,128)(2,1)}), bf16[8,128,1024]{1,2,0:T(8,128)(2,1)}, u32[]{:S(2)}, u32[]{:S(2)}) async-start(bf16[8,128,1024]{1,2,0:T(8,128)(2,1)} %broadcast_in_dim.12), calls=%async_computation | async-start | bytes 4194304 | tf_op jit(solution)/shard_map/all_to_all | solution.py:20
  167.3 2.6 copy.45
  170.0 0.0 copy-done
  170.0 8.1 %abs_reduce_fusion.1 = (f32[1024]{0:T(1024)S(1)}, f32[1024,1024]{0,1:T(8,128)}) fusion(bf16[1024,1024]{0,1:T(8,128)(2,1)} %bitcast.51, f32[1,1,1024,1024]{2,3,1,0:T(8,128)} %copy.43), kind=kOutput, calls=%fused_computation.10 | convolution fusion | flops 2152725504 | bytes 10489856 | tf_op jit(solution)/shard_map/bnm,bnk->bmk/dot_general | solution.py:81
  178.1 0.6 reduce_max.18
  179.4 0.0 copy-start.1
  179.4 3.0 fusion
  182.4 0.4 copy-done.1
  182.8 6.8 %abs_reduce_fusion = (f32[1024]{0:T(1024)S(1)}, f32[1024,1024]{0,1:T(8,128)}) fusion(bf16[8,1,1024,128]{3,2,1,0:T(8,128)(2,1)} %copy-done, f32[1,1,1024,1024]{2,3,1,0:T(8,128)S(1)} %copy-done.1), kind=kOutput, calls=%fused_computation.8 | convolution fusion | flops 2152725504 | bytes 10489856 | tf_op jit(solution)/shard_map/bnm,bkm->bnk/dot_general | solution.py:82
  189.6 0.6 reduce_max.19
  190.9 1.5 fusion.45
  192.5 0.0 copy-start.2
  192.5 5.1 %fusion.29 = bf16[128,1024]{1,0:T(8,128)(2,1)S(1)} fusion(f32[1024,1024]{0,1:T(8,128)} %get-tuple-element.10, f32[]{:T(128)S(6)} %div.20, bf16[128,1024]{1,0:T(8,128)(2,1)S(1)} %fusion.45, s32[128]{0:T(128)S(1)} %iota_add_fusion), kind=kOutput, calls=%fused_computation.23 | convolution fusion | flops 543817728 | bytes 4719108 | tf_op jit(solution)/shard_map/bij,bjk->bik/dot_general | solution.py:44
  197.6 0.0 copy-done.2
  197.6 3.3 fusion.48
  201.0 3.0 fusion.43
  204.1 3.0 fusion.41
  207.1 5.0 %fusion.34 = bf16[128,1024]{1,0:T(8,128)(2,1)S(1)} fusion(bf16[128,1024]{1,0:T(8,128)(2,1)S(1)} %fusion.41, f32[1024,1024]{0,1:T(8,128)} %get-tuple-element.8, f32[]{:T(128)S(6)} %div.21), kind=kOutput, calls=%fused_computation.25 | convolution fusion | flops 547356672 | bytes 4718596 | tf_op jit(solution)/shard_map/bij,bjk->bik/dot_general | solution.py:44
  212.1 5.7 %multiply_reduce_fusion = (f32[]{:T(128)}, f32[128,1024]{1,0:T(8,128)S(1)}) fusion(f32[]{:T(128)S(6)} %mul.123, f32[1024,1024]{0,1:T(8,128)} %get-tuple-element.8, f32[]{:T(128)S(6)} %div.21, bf16[128,1024]{1,0:T(8,128)(2,1)S(1)} %fusion.34, f32[128,1024]{1,0:T(8,128)S(1)} %fusion.43), kind=kOutput, calls=%fused_computation.35 | convolution fusion | flops 543817728 | bytes 5505036 | tf_op jit(solution)/shard_map/bij,bjk->bik/dot_general | solution.py:44
  217.8 0.0 all-to-all-done
  217.8 0.6 broadcast_in_dim.30
  218.4 8.8 %all_to_all.65 = f32[8,1,1]{2,1,0:T(1,128)S(1)} all-to-all(f32[8,1,1]{2,1,0:T(1,128)S(1)} %broadcast_in_dim.30), channel_id=1, replica_groups=mesh['batch'=8,'hidden'=4,'solver'=8] {'solver'}, dimensions={0} | all-to-all | bytes 64 | tf_op jit(solution)/shard_map/all_to_all | solution.py:20
  227.3 7.1 %all-to-all-start.1 = ((bf16[128,32,256]{0,2,1:T(8,128)(2,1)}), bf16[128,32,256]{0,2,1:T(8,128)(2,1)S(1)}, u32[]{:S(2)}, u32[]{:S(2)}) async-start(bf16[128,32,256]{0,2,1:T(8,128)(2,1)} %bitcast.1), calls=%async_computation.1 | async-start | bytes 4194304 | tf_op jit(solution)/shard_map/all_to_all | solution.py:66
  234.3 0.6 reduce_sum.52
  235.7 0.9 subtract_convert_fusion
  236.5 0.2 copy.50
  236.7 47.1 %all-to-all-done.1 = bf16[128,32,256]{0,2,1:T(8,128)(2,1)S(1)} async-done(((bf16[128,32,256]{0,2,1:T(8,128)(2,1)}), bf16[128,32,256]{0,2,1:T(8,128)(2,1)S(1)}, u32[]{:S(2)}, u32[]{:S(2)}) %all-to-all-start.1) | async-done | bytes 2097184 | tf_op jit(solution)/shard_map/all_to_all | solution.py:66
  283.8 1.6 broadcast_in_dim.31
  285.4 4.5 %all-to-all-start.5 = ((bf16[8,128,1024]{1,2,0:T(8,128)(2,1)}), bf16[8,128,1024]{1,2,0:T(8,128)(2,1)}, u32[]{:S(2)}, u32[]{:S(2)}) async-start(bf16[8,128,1024]{1,2,0:T(8,128)(2,1)} %broadcast_in_dim.31), calls=%async_computation.5 | async-start | bytes 4194304 | tf_op jit(solution)/shard_map/all_to_all | solution.py:20
  289.9 0.0 all-gather.3.cloned.1.call-start
  289.9 0.7 all-gather.3.cloned.1.call-update
  290.6 26.6 %all-to-all-done.5 = bf16[8,128,1024]{1,2,0:T(8,128)(2,1)} async-done(((bf16[8,128,1024]{1,2,0:T(8,128)(2,1)}), bf16[8,128,1024]{1,2,0:T(8,128)(2,1)}, u32[]{:S(2)}, u32[]{:S(2)}) %all-to-all-start.5) | async-done | bytes 2097184 | tf_op jit(solution)/shard_map/all_to_all | solution.py:20
  317.2 5.6 %all-to-all-start.6 = ((bf16[128,32,256]{0,2,1:T(8,128)(2,1)}), bf16[128,32,256]{0,2,1:T(8,128)(2,1)}, u32[]{:S(2)}, u32[]{:S(2)}) async-start(bf16[128,32,256]{0,2,1:T(8,128)(2,1)} %bitcast.16), calls=%async_computation.6 | async-start | bytes 4194304 | tf_op jit(solution)/shard_map/all_to_all | solution.py:117
  322.8 2.9 copy.42
  325.7 61.8 %all-gather.3.cloned.1.call-done = bf16[256,4096]{1,0:T(8,128)(2,1)} async-done(((bf16[256,128]{1,0:T(8,128)(2,1)}), bf16[256,4096]{1,0:T(8,128)(2,1)}) %all-gather.3.cloned.1.call-update) | async-done | bytes 2097168 | tf_op jit(solution)/shard_map/all_gather | solution.py:65
  387.6 3.6 convolution_convert_fusion.2
  391.2 1.3 constant_dynamic-slice_fusion
  392.5 1.0 copy.48
  393.5 1.0 copy.46
  394.5 0.0 all-to-all-done.6
  394.5 3.3 copy.51
  397.7 3.0 convolution_convert_fusion.1
  (1 shorter events, 0.0 us)
Async XLA Ops:
  7.2 86.1 %all-gather.5.cloned.1.call-start = ((), (), s32[]{:S(2)}) async-start(), calls=%async_computation.8 | async-start | bytes 4325376 | tf_op jit(solution)/shard_map/all_gather | solution.py:71
  128.3 8.4 %copy-start.3 = (bf16[128,1024]{1,0:T(8,128)(2,1)S(1)}, bf16[128,1024]{1,0:T(8,128)(2,1)}, u32[]{:S(2)}) copy-start(bf16[128,1024]{1,0:T(8,128)(2,1)} %param.7) | copy-start | bytes 786436
  130.3 30.7 %all-to-all-start.3 = ((bf16[8,1,1024,128]{3,2,1,0:T(8,128)(2,1)}), bf16[8,1,1024,128]{3,2,1,0:T(8,128)(2,1)S(1)}, u32[]{:S(2)}, u32[]{:S(2)}) async-start(bf16[8,1,1024,128]{3,2,1,0:T(8,128)(2,1)} %broadcast_in_dim.13), calls=%async_computation.3 | async-start | bytes 4194304 | tf_op jit(solution)/shard_map/all_to_all | solution.py:20
  160.9 9.0 %copy-start = (bf16[8,1,1024,128]{3,2,1,0:T(8,128)(2,1)}, bf16[8,1,1024,128]{3,2,1,0:T(8,128)(2,1)S(1)}, u32[]{:S(2)}) copy-start(bf16[8,1,1024,128]{3,2,1,0:T(8,128)(2,1)S(1)} %all-to-all-done.3) | copy-start | bytes 6291460
  162.8 55.0 %all-to-all-start = ((bf16[8,128,1024]{1,2,0:T(8,128)(2,1)}), bf16[8,128,1024]{1,2,0:T(8,128)(2,1)}, u32[]{:S(2)}, u32[]{:S(2)}) async-start(bf16[8,128,1024]{1,2,0:T(8,128)(2,1)} %broadcast_in_dim.12), calls=%async_computation | async-start | bytes 4194304 | tf_op jit(solution)/shard_map/all_to_all | solution.py:20
  179.4 3.5 copy-start.1
  192.5 5.2 %copy-start.2 = (bf16[1,1024,8,128]{1,3,2,0:T(8,128)(2,1)S(1)}, bf16[1,1024,8,128]{1,3,2,0:T(8,128)(2,1)}, u32[]{:S(2)}) copy-start(bf16[1,1024,8,128]{1,3,2,0:T(8,128)(2,1)} %copy.45) | copy-start | bytes 6291460
  227.3 56.5 %all-to-all-start.1 = ((bf16[128,32,256]{0,2,1:T(8,128)(2,1)}), bf16[128,32,256]{0,2,1:T(8,128)(2,1)S(1)}, u32[]{:S(2)}, u32[]{:S(2)}) async-start(bf16[128,32,256]{0,2,1:T(8,128)(2,1)} %bitcast.1), calls=%async_computation.1 | async-start | bytes 4194304 | tf_op jit(solution)/shard_map/all_to_all | solution.py:66
  285.4 31.8 %all-to-all-start.5 = ((bf16[8,128,1024]{1,2,0:T(8,128)(2,1)}), bf16[8,128,1024]{1,2,0:T(8,128)(2,1)}, u32[]{:S(2)}, u32[]{:S(2)}) async-start(bf16[8,128,1024]{1,2,0:T(8,128)(2,1)} %broadcast_in_dim.31), calls=%async_computation.5 | async-start | bytes 4194304 | tf_op jit(solution)/shard_map/all_to_all | solution.py:20
  289.9 97.7 %all-gather.3.cloned.1.call-start = ((), (), s32[]{:S(2)}) async-start(), calls=%async_computation.7 | async-start | bytes 2162688 | tf_op jit(solution)/shard_map/all_gather | solution.py:65
  317.2 77.3 %all-to-all-start.6 = ((bf16[128,32,256]{0,2,1:T(8,128)(2,1)}), bf16[128,32,256]{0,2,1:T(8,128)(2,1)}, u32[]{:S(2)}, u32[]{:S(2)}) async-start(bf16[128,32,256]{0,2,1:T(8,128)(2,1)} %bitcast.16), calls=%async_computation.6 | async-start | bytes 4194304 | tf_op jit(solution)/shard_map/all_to_all | solution.py:117
Sparse Core Ops, SparseCore 0:
  10.6 82.6 all-gather.4
  293.2 94.3 all-gather.2
where the time goes:
time: 408 us
  waiting for transfers between devices  236 us (58%)
  matrix products  51.7 us (13%)
  blocking collectives  40.4 us (10%)
  local copies, waits for them, and re-layouts  29.3 us (7%)
  starting transfers between devices  28.1 us (7%)
  between operations  16.4 us (4%)
  other arithmetic  6.1 us (1%)
    all_gather x1, waiting for transfers between devices, body(): lax.all_gather(cotangent, ('hidden', 'solver'), axis=0, tiled=True)  85.3 us
    all_gather x1, waiting for transfers between devices, body(): lax.all_gather(activations, ('hidden', 'solver'), axis=1, tiled=True)  61.8 us
    all_to_all x1, waiting for transfers between devices, body(): lax.all_to_all(weight_rows, ('hidden', 'solver'), split_axis=1, concat_ax...  47.1 us
    all_to_all x3, waiting for transfers between devices, sent_to_all(): return lax.all_to_all(copies, axis, split_axis=0, concat_axis=0, tiled=True)  40 us
    all_to_all x1, blocking collectives, summed_on_arrival(): lax.all_to_all(blocks, axis, split_axis=0, concat_axis=0, tiled=True)  31.6 us
    dot_general x6, matrix products, product(): jnp.einsum('bij,bjk->bik', left_mat, right_mat, preferred_element_type=jn...  23.4 us
    all_to_all x3, starting transfers between devices, sent_to_all(): return lax.all_to_all(copies, axis, split_axis=0, concat_axis=0, tiled=True)  15.3 us
    unnamed x11, local copies, waits for them, and re-layouts  11.3 us
  transfers between devices with their start and end apart: 7, of which 5 were waited for; matrix products, arithmetic and copies ran while one was open for 17% of the time, Pallas kernels for 0%

commit v1 on v0

--- a/solution.py
+++ b/solution.py
@@ -7,6 +7,11 @@
 STAT_DECAY = 0.8
 LEARN_RATE = 0.005
 EPSILON = 1e-06
+
+
+def swapped_in(array, axis, dim):
+    sent = jnp.stack([array] * lax.axis_size(axis))
+    return jnp.concatenate(lax.all_to_all(sent, axis, 0, 0), axis=dim)
 
 
 def in_order(blocks, dim):
@@ -68,7 +73,7 @@
     )
     first_sum = transposed_product(weight_cols, gathered)
     first_out = first_sum.astype(jnp.bfloat16)
-    cotangent_all = lax.all_gather(cotangent, ("hidden", "solver"), axis=0, tiled=True)
+    cotangent_all = swapped_in(cotangent, ("hidden", "solver"), 0)
     grad_local = summed_on_arrival(
         jnp.dot(cotangent_all, activations, preferred_element_type=jnp.float32).astype(
             jnp.bfloat16

time: 408 us -> 426 us (1.044)
  blocking collectives: 40.4 us -> 147 us
  waiting for transfers between devices: 236 us -> 150 us
    all_to_all x0 -> x1, blocking collectives: none -> 107 us  [swapped_in(): return jnp.concatenate(lax.all_to_all(sent, axis, 0, 0), axis=dim)]
    all_gather x1 -> x0, waiting for transfers between devices: 85.3 us -> none  [body(): lax.all_gather(cotangent, ('hidden', 'solver'), axis=0, tiled=True)]
    unnamed x11 -> x13, local copies, waits for them, and re-layouts: 11.3 us -> 11.3 us
  transfers between devices with their start and end apart: 7 -> 6, of which waited for: 5 -> 4; matrix products, arithmetic and copies ran while one was open for 17% -> 17% of each run, Pallas kernels for 0% -> 0%
where the time goes in v1:
time: 426 us; the launch traced here: 425 us
  waiting for transfers between devices  150 us (35%)
  blocking collectives  147 us (35%)
  matrix products  49.5 us (12%)
  local copies, waits for them, and re-layouts  30.7 us (7%)
  starting transfers between devices  25.6 us (6%)
  between operations  16.4 us (4%)
  other arithmetic  6.1 us (1%)
    all_to_all x1, blocking collectives, swapped_in(): return jnp.concatenate(lax.all_to_all(sent, axis, 0, 0), axis=dim)  107 us
    all_gather x1, waiting for transfers between devices, body(): lax.all_gather(activations, ('hidden', 'solver'), axis=1, tiled=True)  61.8 us
    all_to_all x1, waiting for transfers between devices, body(): lax.all_to_all(weight_rows, ('hidden', 'solver'), split_axis=1, concat_ax...  47.3 us
    all_to_all x3, waiting for transfers between devices, sent_to_all(): return lax.all_to_all(copies, axis, split_axis=0, concat_axis=0, tiled=True)  40 us
    all_to_all x1, blocking collectives, summed_on_arrival(): lax.all_to_all(blocks, axis, split_axis=0, concat_axis=0, tiled=True)  31.6 us
    dot_general x6, matrix products, product(): jnp.einsum('bij,bjk->bik', left_mat, right_mat, preferred_element_type=jn...  23.4 us
    all_to_all x3, starting transfers between devices, sent_to_all(): return lax.all_to_all(copies, axis, split_axis=0, concat_axis=0, tiled=True)  13.8 us
    unnamed x13, local copies, waits for them, and re-layouts  11.3 us
  transfers between devices with their start and end apart: 6, of which 4 were waited for; matrix products, arithmetic and copies ran while one was open for 17% of the time, Pallas kernels for 0%

profile of v1, /device:TPU:24, one launch (start us, length us, event | category | flops | bytes accessed | tf_op | source)
XLA Modules:
  0.0 425.4 jit_solution(1706377433920125008)
XLA Ops:
  7.2 1.4 stack.2
  8.5 0.0 copy-start.4
  8.6 106.9 %all_to_all.69 = bf16[32,256,256]{2,1,0:T(8,128)(2,1)S(1)} all-to-all(bf16[32,256,256]{2,1,0:T(8,128)(2,1)S(1)} %stack.2), channel_id=1, replica_groups=mesh['batch'=8,'hidden'=4,'solver'=8] {'hidden','solver'}, dimensions={0} | all-to-all | bytes 8388608 | tf_op jit(solution)/shard_map/all_to_all | solution.py:14
  115.4 0.0 copy-done.4
  115.4 1.3 convolution_convert_fusion
  116.7 31.6 %all_to_all.70 = bf16[8,1024,128]{2,1,0:T(8,128)(2,1)S(1)} all-to-all(bf16[8,1024,128]{2,1,0:T(8,128)(2,1)S(1)} %bitcast.50), channel_id=1, replica_groups=mesh['batch'=8,'hidden'=4,'solver'=8] {'batch'}, dimensions={0} | all-to-all | bytes 4194304 | tf_op jit(solution)/shard_map/all_to_all | solution.py:39
  148.3 0.0 copy-start.3
  148.3 0.4 reduce_sum.48
  148.7 1.6 broadcast_in_dim.13
  150.3 4.8 %all-to-all-start.4 = ((bf16[8,1,1024,128]{3,2,1,0:T(8,128)(2,1)}), bf16[8,1,1024,128]{3,2,1,0:T(8,128)(2,1)S(1)}, u32[]{:S(2)}, u32[]{:S(2)}) async-start(bf16[8,1,1024,128]{3,2,1,0:T(8,128)(2,1)} %broadcast_in_dim.13), calls=%async_computation.4 | async-start | bytes 4194304 | tf_op jit(solution)/shard_map/all_to_all | solution.py:25
  155.2 0.0 copy-done.3
  155.2 0.2 copy.41
  155.3 5.4 %copy.43 = f32[1,1,1024,1024]{2,3,1,0:T(8,128)} copy(f32[1,1,1024,1024]{3,2,1,0:T(8,128)} %param.8) | data formatting | bytes 8388608 | tf_op args[3]
  160.7 5.3 %copy.47 = f32[1,1,1024,1024]{2,3,1,0:T(8,128)} copy(f32[1,1,1024,1024]{3,2,1,0:T(8,128)} %param.9) | data formatting | bytes 8388608 | tf_op args[4]
  166.1 13.4 %all-to-all-done.4 = bf16[8,1,1024,128]{3,2,1,0:T(8,128)(2,1)S(1)} async-done(((bf16[8,1,1024,128]{3,2,1,0:T(8,128)(2,1)}), bf16[8,1,1024,128]{3,2,1,0:T(8,128)(2,1)S(1)}, u32[]{:S(2)}, u32[]{:S(2)}) %all-to-all-start.4) | async-done | bytes 2097184 | tf_op jit(solution)/shard_map/all_to_all | solution.py:25
  179.5 0.0 copy-start
  179.5 1.8 broadcast_in_dim.12
  181.3 4.5 %all-to-all-start = ((bf16[8,128,1024]{1,2,0:T(8,128)(2,1)}), bf16[8,128,1024]{1,2,0:T(8,128)(2,1)}, u32[]{:S(2)}, u32[]{:S(2)}) async-start(bf16[8,128,1024]{1,2,0:T(8,128)(2,1)} %broadcast_in_dim.12), calls=%async_computation | async-start | bytes 4194304 | tf_op jit(solution)/shard_map/all_to_all | solution.py:25
  185.9 2.6 copy.45
  188.5 0.0 copy-done
  188.5 8.1 %abs_reduce_fusion.1 = (f32[1024]{0:T(1024)S(1)}, f32[1024,1024]{0,1:T(8,128)}) fusion(bf16[1024,1024]{0,1:T(8,128)(2,1)} %bitcast.53, f32[1,1,1024,1024]{2,3,1,0:T(8,128)} %copy.43), kind=kOutput, calls=%fused_computation.10 | convolution fusion | flops 2152725504 | bytes 10489856 | tf_op jit(solution)/shard_map/bnm,bnk->bmk/dot_general | solution.py:86
  196.6 0.6 reduce_max.18
  198.0 0.0 copy-start.1
  198.0 3.0 fusion
  201.0 0.4 copy-done.1
  201.4 6.8 %abs_reduce_fusion = (f32[1024]{0:T(1024)S(1)}, f32[1024,1024]{0,1:T(8,128)}) fusion(bf16[8,1,1024,128]{3,2,1,0:T(8,128)(2,1)} %copy-done, f32[1,1,1024,1024]{2,3,1,0:T(8,128)S(1)} %copy-done.1), kind=kOutput, calls=%fused_computation.8 | convolution fusion | flops 2152725504 | bytes 10489856 | tf_op jit(solution)/shard_map/bnm,bkm->bnk/dot_general | solution.py:87
  208.2 0.6 reduce_max.19
  209.5 1.5 fusion.45
  211.1 0.0 copy-start.2
  211.1 5.1 %fusion.29 = bf16[128,1024]{1,0:T(8,128)(2,1)S(1)} fusion(f32[1024,1024]{0,1:T(8,128)} %get-tuple-element.10, f32[]{:T(128)S(6)} %div.20, bf16[128,1024]{1,0:T(8,128)(2,1)S(1)} %fusion.45, s32[128]{0:T(128)S(1)} %iota_add_fusion), kind=kOutput, calls=%fused_computation.23 | convolution fusion | flops 543817728 | bytes 4719108 | tf_op jit(solution)/shard_map/bij,bjk->bik/dot_general | solution.py:49
  216.2 0.0 copy-done.2
  216.3 3.3 fusion.48
  219.6 3.0 fusion.43
  222.7 3.0 fusion.41
  225.7 5.0 %fusion.34 = bf16[128,1024]{1,0:T(8,128)(2,1)S(1)} fusion(bf16[128,1024]{1,0:T(8,128)(2,1)S(1)} %fusion.41, f32[1024,1024]{0,1:T(8,128)} %get-tuple-element.8, f32[]{:T(128)S(6)} %div.21), kind=kOutput, calls=%fused_computation.25 | convolution fusion | flops 547356672 | bytes 4718596 | tf_op jit(solution)/shard_map/bij,bjk->bik/dot_general | solution.py:49
  230.7 5.7 %multiply_reduce_fusion = (f32[]{:T(128)}, f32[128,1024]{1,0:T(8,128)S(1)}) fusion(f32[]{:T(128)S(6)} %mul.123, f32[1024,1024]{0,1:T(8,128)} %get-tuple-element.8, f32[]{:T(128)S(6)} %div.21, bf16[128,1024]{1,0:T(8,128)(2,1)S(1)} %fusion.34, f32[128,1024]{1,0:T(8,128)S(1)} %fusion.43), kind=kOutput, calls=%fused_computation.35 | convolution fusion | flops 543817728 | bytes 5505036 | tf_op jit(solution)/shard_map/bij,bjk->bik/dot_general | solution.py:49
  236.4 0.0 all-to-all-done
  236.4 0.6 broadcast_in_dim.30
  237.1 8.8 %all_to_all.71 = f32[8,1,1]{2,1,0:T(1,128)S(1)} all-to-all(f32[8,1,1]{2,1,0:T(1,128)S(1)} %broadcast_in_dim.30), channel_id=1, replica_groups=mesh['batch'=8,'hidden'=4,'solver'=8] {'solver'}, dimensions={0} | all-to-all | bytes 64 | tf_op jit(solution)/shard_map/all_to_all | solution.py:25
  245.9 6.1 %all-to-all-start.1 = ((bf16[128,32,256]{0,2,1:T(8,128)(2,1)}), bf16[128,32,256]{0,2,1:T(8,128)(2,1)S(1)}, u32[]{:S(2)}, u32[]{:S(2)}) async-start(bf16[128,32,256]{0,2,1:T(8,128)(2,1)} %bitcast.1), calls=%async_computation.1 | async-start | bytes 4194304 | tf_op jit(solution)/shard_map/all_to_all | solution.py:71
  252.0 0.6 reduce_sum.52
  253.3 0.9 subtract_convert_fusion
  254.2 0.2 copy.50
  254.4 47.3 %all-to-all-done.1 = bf16[128,32,256]{0,2,1:T(8,128)(2,1)S(1)} async-done(((bf16[128,32,256]{0,2,1:T(8,128)(2,1)}), bf16[128,32,256]{0,2,1:T(8,128)(2,1)S(1)}, u32[]{:S(2)}, u32[]{:S(2)}) %all-to-all-start.1) | async-done | bytes 2097184 | tf_op jit(solution)/shard_map/all_to_all | solution.py:71
  301.7 1.6 broadcast_in_dim.31
  303.3 4.5 %all-to-all-start.6 = ((bf16[8,128,1024]{1,2,0:T(8,128)(2,1)}), bf16[8,128,1024]{1,2,0:T(8,128)(2,1)}, u32[]{:S(2)}, u32[]{:S(2)}) async-start(bf16[8,128,1024]{1,2,0:T(8,128)(2,1)} %broadcast_in_dim.31), calls=%async_computation.6 | async-start | bytes 4194304 | tf_op jit(solution)/shard_map/all_to_all | solution.py:25
  307.7 0.0 all-gather.2.cloned.1.call-start
  307.8 0.7 all-gather.2.cloned.1.call-update
  308.5 26.6 %all-to-all-done.6 = bf16[8,128,1024]{1,2,0:T(8,128)(2,1)} async-done(((bf16[8,128,1024]{1,2,0:T(8,128)(2,1)}), bf16[8,128,1024]{1,2,0:T(8,128)(2,1)}, u32[]{:S(2)}, u32[]{:S(2)}) %all-to-all-start.6) | async-done | bytes 2097184 | tf_op jit(solution)/shard_map/all_to_all | solution.py:25
  335.0 5.6 %all-to-all-start.7 = ((bf16[128,32,256]{0,2,1:T(8,128)(2,1)}), bf16[128,32,256]{0,2,1:T(8,128)(2,1)}, u32[]{:S(2)}, u32[]{:S(2)}) async-start(bf16[128,32,256]{0,2,1:T(8,128)(2,1)} %bitcast.17), calls=%async_computation.7 | async-start | bytes 4194304 | tf_op jit(solution)/shard_map/all_to_all | solution.py:122
  340.7 2.9 copy.42
  343.6 61.8 %all-gather.2.cloned.1.call-done = bf16[256,4096]{1,0:T(8,128)(2,1)} async-done(((bf16[256,128]{1,0:T(8,128)(2,1)}), bf16[256,4096]{1,0:T(8,128)(2,1)}) %all-gather.2.cloned.1.call-update) | async-done | bytes 2097168 | tf_op jit(solution)/shard_map/all_gather | solution.py:70
  405.4 3.6 convolution_convert_fusion.2
  409.0 1.3 constant_dynamic-slice_fusion
  410.3 1.0 copy.48
  411.3 1.0 copy.46
  412.3 0.0 all-to-all-done.7
  412.3 3.3 copy.51
  415.6 3.0 convolution_convert_fusion.1
  (1 shorter events, 0.0 us)
Async XLA Ops:
  8.5 106.9 %copy-start.4 = (bf16[256,128]{1,0:T(8,128)(2,1)S(1)}, bf16[256,128]{1,0:T(8,128)(2,1)}, u32[]{:S(2)}) copy-start(bf16[256,128]{1,0:T(8,128)(2,1)} %param.5) | copy-start | bytes 196612
  148.3 6.9 %copy-start.3 = (bf16[128,1024]{1,0:T(8,128)(2,1)S(1)}, bf16[128,1024]{1,0:T(8,128)(2,1)}, u32[]{:S(2)}) copy-start(bf16[128,1024]{1,0:T(8,128)(2,1)} %param.7) | copy-start | bytes 786436
  150.3 29.2 %all-to-all-start.4 = ((bf16[8,1,1024,128]{3,2,1,0:T(8,128)(2,1)}), bf16[8,1,1024,128]{3,2,1,0:T(8,128)(2,1)S(1)}, u32[]{:S(2)}, u32[]{:S(2)}) async-start(bf16[8,1,1024,128]{3,2,1,0:T(8,128)(2,1)} %broadcast_in_dim.13), calls=%async_computation.4 | async-start | bytes 4194304 | tf_op jit(solution)/shard_map/all_to_all | solution.py:25
  179.5 9.0 %copy-start = (bf16[8,1,1024,128]{3,2,1,0:T(8,128)(2,1)}, bf16[8,1,1024,128]{3,2,1,0:T(8,128)(2,1)S(1)}, u32[]{:S(2)}) copy-start(bf16[8,1,1024,128]{3,2,1,0:T(8,128)(2,1)S(1)} %all-to-all-done.4) | copy-start | bytes 6291460
  181.3 55.1 %all-to-all-start = ((bf16[8,128,1024]{1,2,0:T(8,128)(2,1)}), bf16[8,128,1024]{1,2,0:T(8,128)(2,1)}, u32[]{:S(2)}, u32[]{:S(2)}) async-start(bf16[8,128,1024]{1,2,0:T(8,128)(2,1)} %broadcast_in_dim.12), calls=%async_computation | async-start | bytes 4194304 | tf_op jit(solution)/shard_map/all_to_all | solution.py:25
  198.0 3.5 copy-start.1
  211.1 5.2 %copy-start.2 = (bf16[1,1024,8,128]{1,3,2,0:T(8,128)(2,1)S(1)}, bf16[1,1024,8,128]{1,3,2,0:T(8,128)(2,1)}, u32[]{:S(2)}) copy-start(bf16[1,1024,8,128]{1,3,2,0:T(8,128)(2,1)} %copy.45) | copy-start | bytes 6291460
  245.9 55.8 %all-to-all-start.1 = ((bf16[128,32,256]{0,2,1:T(8,128)(2,1)}), bf16[128,32,256]{0,2,1:T(8,128)(2,1)S(1)}, u32[]{:S(2)}, u32[]{:S(2)}) async-start(bf16[128,32,256]{0,2,1:T(8,128)(2,1)} %bitcast.1), calls=%async_computation.1 | async-start | bytes 4194304 | tf_op jit(solution)/shard_map/all_to_all | solution.py:71
  303.3 31.8 %all-to-all-start.6 = ((bf16[8,128,1024]{1,2,0:T(8,128)(2,1)}), bf16[8,128,1024]{1,2,0:T(8,128)(2,1)}, u32[]{:S(2)}, u32[]{:S(2)}) async-start(bf16[8,128,1024]{1,2,0:T(8,128)(2,1)} %broadcast_in_dim.31), calls=%async_computation.6 | async-start | bytes 4194304 | tf_op jit(solution)/shard_map/all_to_all | solution.py:25
  307.7 97.7 %all-gather.2.cloned.1.call-start = ((), (), s32[]{:S(2)}) async-start(), calls=%async_computation.8 | async-start | bytes 2162688 | tf_op jit(solution)/shard_map/all_gather | solution.py:70
  335.0 77.3 %all-to-all-start.7 = ((bf16[128,32,256]{0,2,1:T(8,128)(2,1)}), bf16[128,32,256]{0,2,1:T(8,128)(2,1)}, u32[]{:S(2)}, u32[]{:S(2)}) async-start(bf16[128,32,256]{0,2,1:T(8,128)(2,1)} %bitcast.17), calls=%async_computation.7 | async-start | bytes 4194304 | tf_op jit(solution)/shard_map/all_to_all | solution.py:122
Sparse Core Ops, SparseCore 0:
  311.0 94.3 all-gather.1
